TPU v7x, 512 devices: a whole 4x8x8 slice. The times are simulated.
512 devices in a mesh: zone: 32 (over x, z_hi, core), period: 16 (over y, z_lo).
Axes of the slice: x: 4, y: 8, z: 8 (z_hi: 4, z_lo: 2; z = z_hi * 2 + z_lo), core: 2. Of those that a mesh axis runs over, the one named last changes fastest.
Arguments:
- x_start: float32 [256, 16, 1600], P('zone', 'period'), may hold values from -6 to 6
- duals: float32 [256, 16, 512], P('zone', 'period'), may hold values from -3 to 3
- cost: float32 [256, 16, 1600], P('zone', 'period'), may hold values from -6 to 6
- hinv: bfloat16 [256, 1600, 1600], P('zone', 'period')
- zone_sizes: int32 [256], P('zone'), may hold values from 640 to 1600, as said below
- partners: int32 [4, 256], P(None, 'zone'), may hold values from 0 to 7, as said below
Outputs:
- primal: float32 [256, 16, 1600], P('zone', 'period')
- dual_out: float32 [256, 16, 512], P('zone', 'period')
Inputs may be any that keep to these rules, and one draw needn't show every extreme that they name: `zone_sizes`: each zone has at least its tie and ramp entries live; some zone uses all 1600. In round r the zones of zone index i are paired one to one with the zones of index i XOR 2**(r mod b), b the log2 of the number of zone indices; partners[r, z] is the partner's position among the 8 zones of its index, and the pairing is mutual.
All inputs are finite; a program needn't handle non-finite values.
Results may differ from a plain program's by a relative error of at most 0.0032.
Values may be sent and summed in bfloat16 or wider, within the bound.
No kernel may reach another device: no remote copies, remote signals or barrier semaphores. Data moves between devices by JAX's collectives and lax.ppermute only.
A program may use at most 64 MiB of HBM per device.

v0:
```python
import jax
import jax.numpy as jnp
from jax import lax
from jax.sharding import PartitionSpec as P

W = 128
G = 128
ROUNDS = 4
ITERS = 2
rho_ties = 1.0
prox_weight = 0.5
ramp_weight = 0.5


def from_partner(block, axis, apart):
    count = lax.axis_size(axis)
    route = []
    for low in range(count):
        high = low | 1 << apart
        if high != low and high < count:
            route += [(low, high), (high, low)]
    return lax.ppermute(block, axis, route)


def padded_2(cells, sides, width):
    for axis, dim in sides:
        count = lax.axis_size(axis)
        ends = count - 1
        head = lax.slice_in_dim(cells, 0, width, axis=dim)
        tail = lax.slice_in_dim(cells, cells.shape[dim] - width, cells.shape[dim], axis=dim)
        cells = jnp.concatenate(
            [
                lax.ppermute(tail, axis, [(i, (i + 1) % count) for i in range(ends)]),
                cells,
                lax.ppermute(head, axis, [((i + 1) % count, i) for i in range(ends)]),
            ],
            axis=dim,
        )
    return cells


def shards(x_start, duals, cost, hinv, zone_sizes, partners):
    zones_here = x_start.shape[0]
    width_total = x_start.shape[2]
    nbits = lax.axis_size("zone").bit_length() - 1
    live_mask = (lax.iota(jnp.int32, width_total)[None, :] < zone_sizes[:, None]).astype(
        jnp.float32
    )[:, None, :]
    tie_end = ROUNDS * W
    current = x_start
    dual_state = duals
    for iteration in range(ITERS):
        tie_terms = []
        new_duals = []
        for round_index in range(ROUNDS):
            own_block = current[:, :, round_index * W : (round_index + 1) * W]
            received = from_partner(own_block, "zone", round_index % nbits)
            partner_block = jnp.take(received, partners[round_index], axis=0)
            old_dual = dual_state[:, :, round_index * W : (round_index + 1) * W]
            updated = old_dual + rho_ties * 0.5 * (own_block - partner_block)
            new_duals.append(updated)
            tie_terms.append(rho_ties * 0.5 * (own_block + partner_block) - updated)
        dual_state = jnp.concatenate(new_duals, axis=2)
        ramp_block = current[:, :, tie_end : tie_end + G]
        padded = padded_2(ramp_block, (("period", 1),), 1)
        ramp_term = ramp_weight * (padded[:, 0:1] + padded[:, 2:3])
        filler = jnp.zeros((zones_here, 1, width_total - tie_end - G), jnp.float32)
        addition = jnp.concatenate(tie_terms + [ramp_term, filler], axis=2)
        right_side = ((prox_weight * current - cost + addition) * live_mask).astype(jnp.bfloat16)
        row_products = jnp.einsum(
            "zpv,zrv->zpr",
            lax.all_gather(right_side, "period", axis=1, tiled=True),
            hinv,
            preferred_element_type=jnp.float32,
        )
        product = lax.all_to_all(row_products, "period", split_axis=1, concat_axis=2, tiled=True)
        current = product * live_mask
    return (current, dual_state)


def solution(mesh):
    placed = (
        P("zone", "period", None),
        P("zone", "period", None),
        P("zone", "period", None),
        P("zone", "period", None),
        P("zone"),
        P(None, "zone"),
    )
    return jax.shard_map(
        shards,
        mesh=mesh,
        in_specs=placed,
        out_specs=(P("zone", "period", None), P("zone", "period", None)),
        check_vma=False,
    )
```

profile of v0, /device:TPU:6, one launch (start us, length us, event | category | flops | bytes accessed | tf_op | source)
XLA Modules:
  0.0 158.9 jit_solution(9922141693585990498)
XLA Ops:
  0.7 1.0 copy.10
  1.6 6.1 %collective-permute-start.1 = (f32[8,1,128]{2,0,1:T(8,128)S(1)}, f32[8,1,128]{2,0,1:T(8,128)S(1)}, u32[]{:S(2)}, u32[]{:S(2)}) collective-permute-start(f32[8,1,128]{2,0,1:T(8,128)S(1)} %get-tuple-element.30), channel_id=1, source_target_pairs={{0,32},{32,0},{16,48},{48,16},{64,96},{96,64},{80,112},{112,80},{1... | collective-permute-start | bytes 12296 | tf_op jit(solution)/shard_map/ppermute | solution.py:22
  7.7 1.9 %collective-permute-start = (f32[8,1,128]{2,0,1:T(8,128)S(1)}, f32[8,1,128]{2,0,1:T(8,128)S(1)}, u32[]{:S(2)}, u32[]{:S(2)}) collective-permute-start(f32[8,1,128]{2,0,1:T(8,128)S(1)} %get-tuple-element.31), channel_id=1, source_target_pairs={{0,16},{16,0},{32,48},{48,32},{64,80},{80,64},{96,112},{112,96},{1... | collective-permute-start | bytes 12296 | tf_op jit(solution)/shard_map/ppermute | solution.py:22
  9.6 0.8 compare_and_fusion
  10.5 0.7 fusion.11
  11.3 0.6 gather_fusion.1
  11.8 0.6 gather_fusion
  12.5 2.7 %collective-permute-start.3 = (f32[8,1,128]{2,0,1:T(8,128)S(1)}, f32[8,1,128]{2,0,1:T(8,128)S(1)}, u32[]{:S(2)}, u32[]{:S(2)}) collective-permute-start(f32[8,1,128]{2,0,1:T(8,128)S(1)} %get-tuple-element.28), channel_id=1, source_target_pairs={{0,128},{128,0},{16,144},{144,16},{32,160},{160,32},{48,176},{176,... | collective-permute-start | bytes 12296 | tf_op jit(solution)/shard_map/ppermute | solution.py:22
  15.3 9.1 %collective-permute-start.2 = (f32[8,1,128]{2,0,1:T(8,128)S(1)}, f32[8,1,128]{2,0,1:T(8,128)S(1)}, u32[]{:S(2)}, u32[]{:S(2)}) collective-permute-start(f32[8,1,128]{2,0,1:T(8,128)S(1)} %get-tuple-element.29), channel_id=1, source_target_pairs={{0,64},{64,0},{16,80},{80,16},{32,96},{96,32},{48,112},{112,48},{1... | collective-permute-start | bytes 12296 | tf_op jit(solution)/shard_map/ppermute | solution.py:22
  24.4 1.3 collective-permute-start.5
  25.7 4.5 %collective-permute-start.4 = (f32[8,1,128]{2,0,1:T(8,128)S(1)}, f32[8,1,128]{2,0,1:T(8,128)S(1)}, u32[]{:S(2)}, u32[]{:S(2)}) collective-permute-start(f32[8,1,128]{2,0,1:T(8,128)S(1)} %get-tuple-element.26), channel_id=1, source_target_pairs={{0,1},{1,2},{2,3},{3,4},{4,5},{5,6},{6,7},{7,8},{8,9},{9,10},{10,1... | collective-permute-start | bytes 12296 | tf_op jit(solution)/shard_map/ppermute | solution.py:33
  30.3 0.6 gather_fusion.3
  30.9 0.6 gather_fusion.2
  31.6 0.9 select_convert_fusion.1
  32.5 37.4 %all_gather.6 = bf16[8,16,1600]{2,0,1:T(8,128)(2,1)S(1)} all-gather(bf16[8,1,1600]{2,0,1:T(8,128)(2,1)S(1)} %select_convert_fusion.1), channel_id=1, replica_groups=mesh['zone'=32,'period'=16] {'period'}, dimensions={1}, use_global_device_ids=true | all-gather | bytes 435200 | tf_op jit(solution)/shard_map/all_gather | solution.py:72
  69.9 0.9 fusion.2
  70.8 15.9 %all_to_all.24 = f32[8,16,100]{2,0,1:T(8,128)S(1)} all-to-all(f32[8,16,100]{2,0,1:T(8,128)S(1)} %copy.23), channel_id=1, replica_groups=mesh['zone'=32,'period'=16] {'period'}, dimensions={1} | all-to-all | bytes 102400 | tf_op jit(solution)/shard_map/all_to_all | solution.py:76
  86.9 2.9 %collective-permute-start.7 = (f32[8,1,128]{2,0,1:T(8,128)S(1)}, f32[8,1,128]{2,0,1:T(8,128)S(1)}, u32[]{:S(2)}, u32[]{:S(2)}) collective-permute-start(f32[8,1,128]{2,0,1:T(8,128)S(1)} %get-tuple-element.24), channel_id=1, source_target_pairs={{0,32},{32,0},{16,48},{48,16},{64,96},{96,64},{80,112},{112,80},{1... | collective-permute-start | bytes 12296 | tf_op jit(solution)/shard_map/ppermute | solution.py:22
  89.8 1.9 %collective-permute-start.6 = (f32[8,1,128]{2,0,1:T(8,128)S(1)}, f32[8,1,128]{2,0,1:T(8,128)S(1)}, u32[]{:S(2)}, u32[]{:S(2)}) collective-permute-start(f32[8,1,128]{2,0,1:T(8,128)S(1)} %get-tuple-element.25), channel_id=1, source_target_pairs={{0,16},{16,0},{32,48},{48,32},{64,80},{80,64},{96,112},{112,96},{1... | collective-permute-start | bytes 12296 | tf_op jit(solution)/shard_map/ppermute | solution.py:22
  91.8 1.6 collective-permute-done.7
  94.6 3.1 %collective-permute-start.9 = (f32[8,1,128]{2,0,1:T(8,128)S(1)}, f32[8,1,128]{2,0,1:T(8,128)S(1)}, u32[]{:S(2)}, u32[]{:S(2)}) collective-permute-start(f32[8,1,128]{2,0,1:T(8,128)S(1)} %get-tuple-element.22), channel_id=1, source_target_pairs={{0,128},{128,0},{16,144},{144,16},{32,160},{160,32},{48,176},{176,... | collective-permute-start | bytes 12296 | tf_op jit(solution)/shard_map/ppermute | solution.py:22
  97.7 1.9 %collective-permute-start.8 = (f32[8,1,128]{2,0,1:T(8,128)S(1)}, f32[8,1,128]{2,0,1:T(8,128)S(1)}, u32[]{:S(2)}, u32[]{:S(2)}) collective-permute-start(f32[8,1,128]{2,0,1:T(8,128)S(1)} %get-tuple-element.23), channel_id=1, source_target_pairs={{0,64},{64,0},{16,80},{80,16},{32,96},{96,32},{48,112},{112,48},{1... | collective-permute-start | bytes 12296 | tf_op jit(solution)/shard_map/ppermute | solution.py:22
  99.6 1.3 collective-permute-start.11
  100.9 4.5 %collective-permute-start.10 = (f32[8,1,128]{2,0,1:T(8,128)S(1)}, f32[8,1,128]{2,0,1:T(8,128)S(1)}, u32[]{:S(2)}, u32[]{:S(2)}) collective-permute-start(f32[8,1,128]{2,0,1:T(8,128)S(1)} %get-tuple-element.21), channel_id=1, source_target_pairs={{0,1},{1,2},{2,3},{3,4},{4,5},{5,6},{6,7},{7,8},{8,9},{9,10},{10,1... | collective-permute-start | bytes 12296 | tf_op jit(solution)/shard_map/ppermute | solution.py:33
  106.1 1.0 collective-permute-done.8
  108.0 33.2 %all_gather.7 = bf16[8,16,1600]{2,0,1:T(8,128)(2,1)S(1)} all-gather(bf16[8,1,1600]{2,0,1:T(8,128)(2,1)S(1)} %select_convert_fusion), channel_id=1, replica_groups=mesh['zone'=32,'period'=16] {'period'}, dimensions={1}, use_global_device_ids=true | all-gather | bytes 435200 | tf_op jit(solution)/shard_map/all_gather | solution.py:72
  141.2 0.9 fusion
  142.0 0.7 copy.28
  142.7 6.3 %all-to-all-start.1 = ((f32[8,16,100]{2,0,1:T(8,128)}), f32[8,16,100]{2,0,1:T(8,128)S(1)}, u32[]{:S(2)}, u32[]{:S(2)}) async-start(f32[8,16,100]{2,0,1:T(8,128)} %copy.28), calls=%async_computation.1 | async-start | bytes 131072 | tf_op jit(solution)/shard_map/all_to_all | solution.py:76
  149.0 0.6 copy.31
  149.6 8.4 %all-to-all-done.1 = f32[8,16,100]{2,0,1:T(8,128)S(1)} async-done(((f32[8,16,100]{2,0,1:T(8,128)}), f32[8,16,100]{2,0,1:T(8,128)S(1)}, u32[]{:S(2)}, u32[]{:S(2)}) %all-to-all-start.1) | async-done | bytes 51232 | tf_op jit(solution)/shard_map/all_to_all | solution.py:76
  158.2 0.7 copy.30
  (46 shorter events, 3.4 us)
Async XLA Ops:
  0.6 69.3 %copy-start = (bf16[8,100,1600]{2,0,1:T(8,128)(2,1)S(1)}, bf16[8,100,1600]{2,0,1:T(8,128)(2,1)}, u32[]{:S(2)}) copy-start(bf16[8,100,1600]{2,0,1:T(8,128)(2,1)} %param.11) | copy-start | bytes 7680004
  0.6 86.2 %copy-start.2 = (s32[8]{0:T(128)S(1)}, s32[8]{0:T(128)}, u32[]{:S(2)}) copy-start(s32[8]{0:T(128)} %param.12) | copy-start | bytes 100
  1.6 9.6 %collective-permute-start.1 = (f32[8,1,128]{2,0,1:T(8,128)S(1)}, f32[8,1,128]{2,0,1:T(8,128)S(1)}, u32[]{:S(2)}, u32[]{:S(2)}) collective-permute-start(f32[8,1,128]{2,0,1:T(8,128)S(1)} %get-tuple-element.30), channel_id=1, source_target_pairs={{0,32},{32,0},{16,48},{48,16},{64,96},{96,64},{80,112},{112,80},{1... | collective-permute-start | bytes 12296 | tf_op jit(solution)/shard_map/ppermute | solution.py:22
  7.7 4.1 %collective-permute-start = (f32[8,1,128]{2,0,1:T(8,128)S(1)}, f32[8,1,128]{2,0,1:T(8,128)S(1)}, u32[]{:S(2)}, u32[]{:S(2)}) collective-permute-start(f32[8,1,128]{2,0,1:T(8,128)S(1)} %get-tuple-element.31), channel_id=1, source_target_pairs={{0,16},{16,0},{32,48},{48,32},{64,80},{80,64},{96,112},{112,96},{1... | collective-permute-start | bytes 12296 | tf_op jit(solution)/shard_map/ppermute | solution.py:22
  11.8 96.0 %copy-start.1 = (f32[8,1,1600]{2,1,0:T(1,128)S(1)}, f32[8,1,1600]{2,1,0:T(1,128)}, u32[]{:S(2)}) copy-start(f32[8,1,1600]{2,1,0:T(1,128)} %param.10) | copy-start | bytes 153604
  12.5 17.7 %collective-permute-start.3 = (f32[8,1,128]{2,0,1:T(8,128)S(1)}, f32[8,1,128]{2,0,1:T(8,128)S(1)}, u32[]{:S(2)}, u32[]{:S(2)}) collective-permute-start(f32[8,1,128]{2,0,1:T(8,128)S(1)} %get-tuple-element.28), channel_id=1, source_target_pairs={{0,128},{128,0},{16,144},{144,16},{32,160},{160,32},{48,176},{176,... | collective-permute-start | bytes 12296 | tf_op jit(solution)/shard_map/ppermute | solution.py:22
  15.3 15.6 %collective-permute-start.2 = (f32[8,1,128]{2,0,1:T(8,128)S(1)}, f32[8,1,128]{2,0,1:T(8,128)S(1)}, u32[]{:S(2)}, u32[]{:S(2)}) collective-permute-start(f32[8,1,128]{2,0,1:T(8,128)S(1)} %get-tuple-element.29), channel_id=1, source_target_pairs={{0,64},{64,0},{16,80},{80,16},{32,96},{96,32},{48,112},{112,48},{1... | collective-permute-start | bytes 12296 | tf_op jit(solution)/shard_map/ppermute | solution.py:22
  24.4 7.1 %collective-permute-start.5 = (f32[8,1,128]{2,0,1:T(8,128)S(1)}, f32[8,1,128]{2,0,1:T(8,128)S(1)}, u32[]{:S(2)}, u32[]{:S(2)}) collective-permute-start(f32[8,1,128]{2,0,1:T(8,128)S(1)} %get-tuple-element.26), channel_id=1, source_target_pairs={{1,0},{2,1},{3,2},{4,3},{5,4},{6,5},{7,6},{8,7},{9,8},{10,9},{11,1... | collective-permute-start | bytes 12296 | tf_op jit(solution)/shard_map/ppermute | solution.py:35
  25.7 5.9 %collective-permute-start.4 = (f32[8,1,128]{2,0,1:T(8,128)S(1)}, f32[8,1,128]{2,0,1:T(8,128)S(1)}, u32[]{:S(2)}, u32[]{:S(2)}) collective-permute-start(f32[8,1,128]{2,0,1:T(8,128)S(1)} %get-tuple-element.26), channel_id=1, source_target_pairs={{0,1},{1,2},{2,3},{3,4},{4,5},{5,6},{6,7},{7,8},{8,9},{9,10},{10,1... | collective-permute-start | bytes 12296 | tf_op jit(solution)/shard_map/ppermute | solution.py:33
  86.9 6.4 %collective-permute-start.7 = (f32[8,1,128]{2,0,1:T(8,128)S(1)}, f32[8,1,128]{2,0,1:T(8,128)S(1)}, u32[]{:S(2)}, u32[]{:S(2)}) collective-permute-start(f32[8,1,128]{2,0,1:T(8,128)S(1)} %get-tuple-element.24), channel_id=1, source_target_pairs={{0,32},{32,0},{16,48},{48,16},{64,96},{96,64},{80,112},{112,80},{1... | collective-permute-start | bytes 12296 | tf_op jit(solution)/shard_map/ppermute | solution.py:22
  89.8 4.1 %collective-permute-start.6 = (f32[8,1,128]{2,0,1:T(8,128)S(1)}, f32[8,1,128]{2,0,1:T(8,128)S(1)}, u32[]{:S(2)}, u32[]{:S(2)}) collective-permute-start(f32[8,1,128]{2,0,1:T(8,128)S(1)} %get-tuple-element.25), channel_id=1, source_target_pairs={{0,16},{16,0},{32,48},{48,32},{64,80},{80,64},{96,112},{112,96},{1... | collective-permute-start | bytes 12296 | tf_op jit(solution)/shard_map/ppermute | solution.py:22
  94.6 10.9 %collective-permute-start.9 = (f32[8,1,128]{2,0,1:T(8,128)S(1)}, f32[8,1,128]{2,0,1:T(8,128)S(1)}, u32[]{:S(2)}, u32[]{:S(2)}) collective-permute-start(f32[8,1,128]{2,0,1:T(8,128)S(1)} %get-tuple-element.22), channel_id=1, source_target_pairs={{0,128},{128,0},{16,144},{144,16},{32,160},{160,32},{48,176},{176,... | collective-permute-start | bytes 12296 | tf_op jit(solution)/shard_map/ppermute | solution.py:22
  97.7 9.4 %collective-permute-start.8 = (f32[8,1,128]{2,0,1:T(8,128)S(1)}, f32[8,1,128]{2,0,1:T(8,128)S(1)}, u32[]{:S(2)}, u32[]{:S(2)}) collective-permute-start(f32[8,1,128]{2,0,1:T(8,128)S(1)} %get-tuple-element.23), channel_id=1, source_target_pairs={{0,64},{64,0},{16,80},{80,16},{32,96},{96,32},{48,112},{112,48},{1... | collective-permute-start | bytes 12296 | tf_op jit(solution)/shard_map/ppermute | solution.py:22
  99.6 8.2 %collective-permute-start.11 = (f32[8,1,128]{2,0,1:T(8,128)S(1)}, f32[8,1,128]{2,0,1:T(8,128)S(1)}, u32[]{:S(2)}, u32[]{:S(2)}) collective-permute-start(f32[8,1,128]{2,0,1:T(8,128)S(1)} %get-tuple-element.21), channel_id=1, source_target_pairs={{1,0},{2,1},{3,2},{4,3},{5,4},{6,5},{7,6},{8,7},{9,8},{10,9},{11,1... | collective-permute-start | bytes 12296 | tf_op jit(solution)/shard_map/ppermute | solution.py:35
  100.9 6.9 %collective-permute-start.10 = (f32[8,1,128]{2,0,1:T(8,128)S(1)}, f32[8,1,128]{2,0,1:T(8,128)S(1)}, u32[]{:S(2)}, u32[]{:S(2)}) collective-permute-start(f32[8,1,128]{2,0,1:T(8,128)S(1)} %get-tuple-element.21), channel_id=1, source_target_pairs={{0,1},{1,2},{2,3},{3,4},{4,5},{5,6},{6,7},{7,8},{8,9},{9,10},{10,1... | collective-permute-start | bytes 12296 | tf_op jit(solution)/shard_map/ppermute | solution.py:33
  142.7 15.3 %all-to-all-start.1 = ((f32[8,16,100]{2,0,1:T(8,128)}), f32[8,16,100]{2,0,1:T(8,128)S(1)}, u32[]{:S(2)}, u32[]{:S(2)}) async-start(f32[8,16,100]{2,0,1:T(8,128)} %copy.28), calls=%async_computation.1 | async-start | bytes 131072 | tf_op jit(solution)/shard_map/all_to_all | solution.py:76
where the time goes:
time: 160 us; the launch traced here: 159 us
  blocking collectives  86.5 us (54%)
  starting transfers between devices  47.6 us (30%)
  waiting for transfers between devices  11.1 us (7%)
  local copies, waits for them, and re-layouts  8.4 us (5%)
  other arithmetic  2.66 us (2%)
  matrix products  1.75 us (1%)
    all_gather x2, blocking collectives, shards(): lax.all_gather(right_side, 'period', axis=1, tiled=True)  70.6 us
    ppermute x8, starting transfers between devices, from_partner(): return lax.ppermute(block, axis, route)  29.7 us
    all_to_all x1, blocking collectives, shards(): lax.all_to_all(row_products, 'period', split_axis=1, concat_axis=2, tiled...  15.9 us
    ppermute x2, starting transfers between devices, padded_2(): lax.ppermute(tail, axis, [(i, (i + 1) % count) for i in range(ends)])  9.09 us
    all_to_all x1, waiting for transfers between devices, shards(): lax.all_to_all(row_products, 'period', split_axis=1, concat_axis=2, tiled...  8.41 us
    all_to_all x1, starting transfers between devices, shards(): lax.all_to_all(row_products, 'period', split_axis=1, concat_axis=2, tiled...  6.28 us
    gather x8, local copies, waits for them, and re-layouts, shards(): partner_block = jnp.take(received, partners[round_index], axis=0)  4.44 us
  transfers between devices with their start and end apart: 13, of which 3 were waited for; matrix products, arithmetic and copies ran while one was open for 4% of the time, Pallas kernels for 0%

commit v1 on v0

--- a/solution.py
+++ b/solution.py
@@ -69,7 +69,10 @@
         right_side = ((prox_weight * current - cost + addition) * live_mask).astype(jnp.bfloat16)
         row_products = jnp.einsum(
             "zpv,zrv->zpr",
-            lax.all_gather(right_side, "period", axis=1, tiled=True),
+            jnp.concatenate(
+                lax.all_to_all(jnp.stack([right_side] * lax.axis_size("period")), "period", 0, 0),
+                axis=1,
+            ),
             hinv,
             preferred_element_type=jnp.float32,
         )

time: 160 us -> 126 us (0.79)
  blocking collectives: 86.5 us -> 55 us
  starting transfers between devices: 47.6 us -> 44.7 us
    all_gather x2 -> x0, blocking collectives: 70.6 us -> none  [shards(): lax.all_gather(right_side, 'period', axis=1, tiled=True)]
    all_to_all x0 -> x2, blocking collectives: none -> 43.4 us  [shards(): lax.all_to_all(jnp.stack([right_side] * lax.axis_size('period')), 'period...]
    all_to_all x1, blocking collectives: 15.9 us -> 11.7 us  [shards(): lax.all_to_all(row_products, 'period', split_axis=1, concat_axis=2, tiled...]
    all_to_all x1, starting transfers between devices: 6.28 us -> 3.5 us  [shards(): lax.all_to_all(row_products, 'period', split_axis=1, concat_axis=2, tiled...]
  transfers between devices with their start and end apart: 13 -> 13, of which waited for: 3 -> 3; matrix products, arithmetic and copies ran while one was open for 4% -> 5% of each run, Pallas kernels for 0% -> 0%
where the time goes in v1:
time: 126 us; the launch traced here: 125 us
  blocking collectives  55 us (44%)
  starting transfers between devices  44.7 us (35%)
  waiting for transfers between devices  11.3 us (9%)
  local copies, waits for them, and re-layouts  8.46 us (7%)
  other arithmetic  2.66 us (2%)
  matrix products  1.75 us (1%)
    all_to_all x2, blocking collectives, shards(): lax.all_to_all(jnp.stack([right_side] * lax.axis_size('period')), 'period...  43.4 us
    ppermute x8, starting transfers between devices, from_partner(): return lax.ppermute(block, axis, route)  29.5 us
    all_to_all x1, blocking collectives, shards(): lax.all_to_all(row_products, 'period', split_axis=1, concat_axis=2, tiled...  11.7 us
    ppermute x2, starting transfers between devices, padded_2(): lax.ppermute(tail, axis, [(i, (i + 1) % count) for i in range(ends)])  9.09 us
    all_to_all x1, waiting for transfers between devices, shards(): lax.all_to_all(row_products, 'period', split_axis=1, concat_axis=2, tiled...  8.42 us
    gather x8, local copies, waits for them, and re-layouts, shards(): partner_block = jnp.take(received, partners[round_index], axis=0)  4.44 us
    all_to_all x1, starting transfers between devices, shards(): lax.all_to_all(row_products, 'period', split_axis=1, concat_axis=2, tiled...  3.5 us
    ppermute x8, waiting for transfers between devices, from_partner(): return lax.ppermute(block, axis, route)  2.81 us
  transfers between devices with their start and end apart: 13, of which 3 were waited for; matrix products, arithmetic and copies ran while one was open for 5% of the time, Pallas kernels for 0%

profile of v1, /device:TPU:6, one launch (start us, length us, event | category | flops | bytes accessed | tf_op | source)
XLA Modules:
  0.0 124.8 jit_solution(7314195584377905940)
XLA Ops:
  0.6 1.0 copy.24
  1.6 6.1 %collective-permute-start.1 = (f32[8,1,128]{2,0,1:T(8,128)S(1)}, f32[8,1,128]{2,0,1:T(8,128)S(1)}, u32[]{:S(2)}, u32[]{:S(2)}) collective-permute-start(f32[8,1,128]{2,0,1:T(8,128)S(1)} %get-tuple-element.32), channel_id=1, source_target_pairs={{0,32},{32,0},{16,48},{48,16},{64,96},{96,64},{80,112},{112,80},{1... | collective-permute-start | bytes 12296 | tf_op jit(solution)/shard_map/ppermute | solution.py:22
  7.7 1.9 %collective-permute-start = (f32[8,1,128]{2,0,1:T(8,128)S(1)}, f32[8,1,128]{2,0,1:T(8,128)S(1)}, u32[]{:S(2)}, u32[]{:S(2)}) collective-permute-start(f32[8,1,128]{2,0,1:T(8,128)S(1)} %get-tuple-element.33), channel_id=1, source_target_pairs={{0,16},{16,0},{32,48},{48,32},{64,80},{80,64},{96,112},{112,96},{1... | collective-permute-start | bytes 12296 | tf_op jit(solution)/shard_map/ppermute | solution.py:22
  9.6 0.8 compare_and_fusion
  10.5 0.7 fusion.15
  11.2 0.6 gather_fusion.1
  11.8 0.6 gather_fusion
  12.5 2.7 %collective-permute-start.3 = (f32[8,1,128]{2,0,1:T(8,128)S(1)}, f32[8,1,128]{2,0,1:T(8,128)S(1)}, u32[]{:S(2)}, u32[]{:S(2)}) collective-permute-start(f32[8,1,128]{2,0,1:T(8,128)S(1)} %get-tuple-element.30), channel_id=1, source_target_pairs={{0,128},{128,0},{16,144},{144,16},{32,160},{160,32},{48,176},{176,... | collective-permute-start | bytes 12296 | tf_op jit(solution)/shard_map/ppermute | solution.py:22
  15.3 9.1 %collective-permute-start.2 = (f32[8,1,128]{2,0,1:T(8,128)S(1)}, f32[8,1,128]{2,0,1:T(8,128)S(1)}, u32[]{:S(2)}, u32[]{:S(2)}) collective-permute-start(f32[8,1,128]{2,0,1:T(8,128)S(1)} %get-tuple-element.31), channel_id=1, source_target_pairs={{0,64},{64,0},{16,80},{80,16},{32,96},{96,32},{48,112},{112,48},{1... | collective-permute-start | bytes 12296 | tf_op jit(solution)/shard_map/ppermute | solution.py:22
  24.4 1.3 %collective-permute-start.5 = (f32[8,1,128]{2,0,1:T(8,128)S(1)}, f32[8,1,128]{2,0,1:T(8,128)S(1)}, u32[]{:S(2)}, u32[]{:S(2)}) collective-permute-start(f32[8,1,128]{2,0,1:T(8,128)S(1)} %get-tuple-element.28), channel_id=1, source_target_pairs={{1,0},{2,1},{3,2},{4,3},{5,4},{6,5},{7,6},{8,7},{9,8},{10,9},{11,1... | collective-permute-start | bytes 12296 | tf_op jit(solution)/shard_map/ppermute | solution.py:35
  25.7 4.5 %collective-permute-start.4 = (f32[8,1,128]{2,0,1:T(8,128)S(1)}, f32[8,1,128]{2,0,1:T(8,128)S(1)}, u32[]{:S(2)}, u32[]{:S(2)}) collective-permute-start(f32[8,1,128]{2,0,1:T(8,128)S(1)} %get-tuple-element.28), channel_id=1, source_target_pairs={{0,1},{1,2},{2,3},{3,4},{4,5},{5,6},{6,7},{7,8},{8,9},{9,10},{10,1... | collective-permute-start | bytes 12296 | tf_op jit(solution)/shard_map/ppermute | solution.py:33
  30.8 0.6 gather_fusion.2
  31.6 0.9 fusion.10
  32.6 24.9 %all_to_all.34 = bf16[16,8,1,1600]{3,1,2,0:T(8,128)(2,1)S(1)} all-to-all(bf16[16,8,1,1600]{3,1,2,0:T(8,128)(2,1)S(1)} %stack.4), channel_id=1, replica_groups=mesh['zone'=32,'period'=16] {'period'}, dimensions={0} | all-to-all | bytes 819200 | tf_op jit(solution)/shard_map/all_to_all | solution.py:73
  57.4 0.9 fusion.2
  58.3 11.7 %all_to_all.35 = f32[8,16,100]{2,0,1:T(8,128)S(1)} all-to-all(f32[8,16,100]{2,0,1:T(8,128)S(1)} %copy.37), channel_id=1, replica_groups=mesh['zone'=32,'period'=16] {'period'}, dimensions={1} | all-to-all | bytes 102400 | tf_op jit(solution)/shard_map/all_to_all | solution.py:79
  70.2 2.4 %collective-permute-start.7 = (f32[8,1,128]{2,0,1:T(8,128)S(1)}, f32[8,1,128]{2,0,1:T(8,128)S(1)}, u32[]{:S(2)}, u32[]{:S(2)}) collective-permute-start(f32[8,1,128]{2,0,1:T(8,128)S(1)} %get-tuple-element.26), channel_id=1, source_target_pairs={{0,32},{32,0},{16,48},{48,16},{64,96},{96,64},{80,112},{112,80},{1... | collective-permute-start | bytes 12296 | tf_op jit(solution)/shard_map/ppermute | solution.py:22
  72.6 1.9 %collective-permute-start.6 = (f32[8,1,128]{2,0,1:T(8,128)S(1)}, f32[8,1,128]{2,0,1:T(8,128)S(1)}, u32[]{:S(2)}, u32[]{:S(2)}) collective-permute-start(f32[8,1,128]{2,0,1:T(8,128)S(1)} %get-tuple-element.27), channel_id=1, source_target_pairs={{0,16},{16,0},{32,48},{48,32},{64,80},{80,64},{96,112},{112,96},{1... | collective-permute-start | bytes 12296 | tf_op jit(solution)/shard_map/ppermute | solution.py:22
  74.6 2.0 %collective-permute-done.7 = f32[8,1,128]{2,0,1:T(8,128)S(1)} collective-permute-done((f32[8,1,128]{2,0,1:T(8,128)S(1)}, f32[8,1,128]{2,0,1:T(8,128)S(1)}, u32[]{:S(2)}, u32[]{:S(2)}) %collective-permute-start.7) | collective-permute-done | bytes 4128 | tf_op jit(solution)/shard_map/ppermute | solution.py:22
  77.2 0.6 gather_fusion.4
  77.9 3.1 %collective-permute-start.9 = (f32[8,1,128]{2,0,1:T(8,128)S(1)}, f32[8,1,128]{2,0,1:T(8,128)S(1)}, u32[]{:S(2)}, u32[]{:S(2)}) collective-permute-start(f32[8,1,128]{2,0,1:T(8,128)S(1)} %get-tuple-element.24), channel_id=1, source_target_pairs={{0,128},{128,0},{16,144},{144,16},{32,160},{160,32},{48,176},{176,... | collective-permute-start | bytes 12296 | tf_op jit(solution)/shard_map/ppermute | solution.py:22
  81.0 2.2 %collective-permute-start.8 = (f32[8,1,128]{2,0,1:T(8,128)S(1)}, f32[8,1,128]{2,0,1:T(8,128)S(1)}, u32[]{:S(2)}, u32[]{:S(2)}) collective-permute-start(f32[8,1,128]{2,0,1:T(8,128)S(1)} %get-tuple-element.25), channel_id=1, source_target_pairs={{0,64},{64,0},{16,80},{80,16},{32,96},{96,32},{48,112},{112,48},{1... | collective-permute-start | bytes 12296 | tf_op jit(solution)/shard_map/ppermute | solution.py:22
  83.2 1.3 %collective-permute-start.11 = (f32[8,1,128]{2,0,1:T(8,128)S(1)}, f32[8,1,128]{2,0,1:T(8,128)S(1)}, u32[]{:S(2)}, u32[]{:S(2)}) collective-permute-start(f32[8,1,128]{2,0,1:T(8,128)S(1)} %get-tuple-element.23), channel_id=1, source_target_pairs={{1,0},{2,1},{3,2},{4,3},{5,4},{6,5},{7,6},{8,7},{9,8},{10,9},{11,1... | collective-permute-start | bytes 12296 | tf_op jit(solution)/shard_map/ppermute | solution.py:35
  84.5 4.5 %collective-permute-start.10 = (f32[8,1,128]{2,0,1:T(8,128)S(1)}, f32[8,1,128]{2,0,1:T(8,128)S(1)}, u32[]{:S(2)}, u32[]{:S(2)}) collective-permute-start(f32[8,1,128]{2,0,1:T(8,128)S(1)} %get-tuple-element.23), channel_id=1, source_target_pairs={{0,1},{1,2},{2,3},{3,4},{4,5},{5,6},{6,7},{7,8},{8,9},{9,10},{10,1... | collective-permute-start | bytes 12296 | tf_op jit(solution)/shard_map/ppermute | solution.py:33
  89.6 0.8 collective-permute-done.8
  91.3 18.5 %all_to_all.36 = bf16[16,8,1,1600]{3,1,2,0:T(8,128)(2,1)S(1)} all-to-all(bf16[16,8,1,1600]{3,1,2,0:T(8,128)(2,1)S(1)} %stack.5), channel_id=1, replica_groups=mesh['zone'=32,'period'=16] {'period'}, dimensions={0} | all-to-all | bytes 819200 | tf_op jit(solution)/shard_map/all_to_all | solution.py:73
  109.8 0.9 fusion
  110.7 0.7 copy.42
  111.3 3.5 %all-to-all-start.3 = ((f32[8,16,100]{2,0,1:T(8,128)}), f32[8,16,100]{2,0,1:T(8,128)S(1)}, u32[]{:S(2)}, u32[]{:S(2)}) async-start(f32[8,16,100]{2,0,1:T(8,128)} %copy.42), calls=%async_computation.3 | async-start | bytes 131072 | tf_op jit(solution)/shard_map/all_to_all | solution.py:79
  114.8 0.6 copy.45
  115.5 8.4 %all-to-all-done.3 = f32[8,16,100]{2,0,1:T(8,128)S(1)} async-done(((f32[8,16,100]{2,0,1:T(8,128)}), f32[8,16,100]{2,0,1:T(8,128)S(1)}, u32[]{:S(2)}, u32[]{:S(2)}) %all-to-all-start.3) | async-done | bytes 51232 | tf_op jit(solution)/shard_map/all_to_all | solution.py:79
  124.1 0.7 copy.44
  (48 shorter events, 3.5 us)
Async XLA Ops:
  0.6 56.8 %copy-start = (bf16[8,100,1600]{2,0,1:T(8,128)(2,1)S(1)}, bf16[8,100,1600]{2,0,1:T(8,128)(2,1)}, u32[]{:S(2)}) copy-start(bf16[8,100,1600]{2,0,1:T(8,128)(2,1)} %param.11) | copy-start | bytes 7680004
  1.6 9.6 %collective-permute-start.1 = (f32[8,1,128]{2,0,1:T(8,128)S(1)}, f32[8,1,128]{2,0,1:T(8,128)S(1)}, u32[]{:S(2)}, u32[]{:S(2)}) collective-permute-start(f32[8,1,128]{2,0,1:T(8,128)S(1)} %get-tuple-element.32), channel_id=1, source_target_pairs={{0,32},{32,0},{16,48},{48,16},{64,96},{96,64},{80,112},{112,80},{1... | collective-permute-start | bytes 12296 | tf_op jit(solution)/shard_map/ppermute | solution.py:22
  7.7 4.1 %collective-permute-start = (f32[8,1,128]{2,0,1:T(8,128)S(1)}, f32[8,1,128]{2,0,1:T(8,128)S(1)}, u32[]{:S(2)}, u32[]{:S(2)}) collective-permute-start(f32[8,1,128]{2,0,1:T(8,128)S(1)} %get-tuple-element.33), channel_id=1, source_target_pairs={{0,16},{16,0},{32,48},{48,32},{64,80},{80,64},{96,112},{112,96},{1... | collective-permute-start | bytes 12296 | tf_op jit(solution)/shard_map/ppermute | solution.py:22
  12.5 17.7 %collective-permute-start.3 = (f32[8,1,128]{2,0,1:T(8,128)S(1)}, f32[8,1,128]{2,0,1:T(8,128)S(1)}, u32[]{:S(2)}, u32[]{:S(2)}) collective-permute-start(f32[8,1,128]{2,0,1:T(8,128)S(1)} %get-tuple-element.30), channel_id=1, source_target_pairs={{0,128},{128,0},{16,144},{144,16},{32,160},{160,32},{48,176},{176,... | collective-permute-start | bytes 12296 | tf_op jit(solution)/shard_map/ppermute | solution.py:22
  15.3 15.6 %collective-permute-start.2 = (f32[8,1,128]{2,0,1:T(8,128)S(1)}, f32[8,1,128]{2,0,1:T(8,128)S(1)}, u32[]{:S(2)}, u32[]{:S(2)}) collective-permute-start(f32[8,1,128]{2,0,1:T(8,128)S(1)} %get-tuple-element.31), channel_id=1, source_target_pairs={{0,64},{64,0},{16,80},{80,16},{32,96},{96,32},{48,112},{112,48},{1... | collective-permute-start | bytes 12296 | tf_op jit(solution)/shard_map/ppermute | solution.py:22
  24.4 7.1 %collective-permute-start.5 = (f32[8,1,128]{2,0,1:T(8,128)S(1)}, f32[8,1,128]{2,0,1:T(8,128)S(1)}, u32[]{:S(2)}, u32[]{:S(2)}) collective-permute-start(f32[8,1,128]{2,0,1:T(8,128)S(1)} %get-tuple-element.28), channel_id=1, source_target_pairs={{1,0},{2,1},{3,2},{4,3},{5,4},{6,5},{7,6},{8,7},{9,8},{10,9},{11,1... | collective-permute-start | bytes 12296 | tf_op jit(solution)/shard_map/ppermute | solution.py:35
  25.7 5.9 %collective-permute-start.4 = (f32[8,1,128]{2,0,1:T(8,128)S(1)}, f32[8,1,128]{2,0,1:T(8,128)S(1)}, u32[]{:S(2)}, u32[]{:S(2)}) collective-permute-start(f32[8,1,128]{2,0,1:T(8,128)S(1)} %get-tuple-element.28), channel_id=1, source_target_pairs={{0,1},{1,2},{2,3},{3,4},{4,5},{5,6},{6,7},{7,8},{8,9},{9,10},{10,1... | collective-permute-start | bytes 12296 | tf_op jit(solution)/shard_map/ppermute | solution.py:33
  31.6 38.5 %copy-start.2 = (s32[8]{0:T(128)S(1)}, s32[8]{0:T(128)}, u32[]{:S(2)}) copy-start(s32[8]{0:T(128)} %param.12) | copy-start | bytes 100
  32.6 58.6 %copy-start.1 = (f32[8,1,1600]{2,1,0:T(1,128)S(1)}, f32[8,1,1600]{2,1,0:T(1,128)}, u32[]{:S(2)}) copy-start(f32[8,1,1600]{2,1,0:T(1,128)} %param.10) | copy-start | bytes 153604
  70.2 6.4 %collective-permute-start.7 = (f32[8,1,128]{2,0,1:T(8,128)S(1)}, f32[8,1,128]{2,0,1:T(8,128)S(1)}, u32[]{:S(2)}, u32[]{:S(2)}) collective-permute-start(f32[8,1,128]{2,0,1:T(8,128)S(1)} %get-tuple-element.26), channel_id=1, source_target_pairs={{0,32},{32,0},{16,48},{48,16},{64,96},{96,64},{80,112},{112,80},{1... | collective-permute-start | bytes 12296 | tf_op jit(solution)/shard_map/ppermute | solution.py:22
  72.6 4.5 %collective-permute-start.6 = (f32[8,1,128]{2,0,1:T(8,128)S(1)}, f32[8,1,128]{2,0,1:T(8,128)S(1)}, u32[]{:S(2)}, u32[]{:S(2)}) collective-permute-start(f32[8,1,128]{2,0,1:T(8,128)S(1)} %get-tuple-element.27), channel_id=1, source_target_pairs={{0,16},{16,0},{32,48},{48,32},{64,80},{80,64},{96,112},{112,96},{1... | collective-permute-start | bytes 12296 | tf_op jit(solution)/shard_map/ppermute | solution.py:22
  77.9 11.2 %collective-permute-start.9 = (f32[8,1,128]{2,0,1:T(8,128)S(1)}, f32[8,1,128]{2,0,1:T(8,128)S(1)}, u32[]{:S(2)}, u32[]{:S(2)}) collective-permute-start(f32[8,1,128]{2,0,1:T(8,128)S(1)} %get-tuple-element.24), channel_id=1, source_target_pairs={{0,128},{128,0},{16,144},{144,16},{32,160},{160,32},{48,176},{176,... | collective-permute-start | bytes 12296 | tf_op jit(solution)/shard_map/ppermute | solution.py:22
  81.0 9.4 %collective-permute-start.8 = (f32[8,1,128]{2,0,1:T(8,128)S(1)}, f32[8,1,128]{2,0,1:T(8,128)S(1)}, u32[]{:S(2)}, u32[]{:S(2)}) collective-permute-start(f32[8,1,128]{2,0,1:T(8,128)S(1)} %get-tuple-element.25), channel_id=1, source_target_pairs={{0,64},{64,0},{16,80},{80,16},{32,96},{96,32},{48,112},{112,48},{1... | collective-permute-start | bytes 12296 | tf_op jit(solution)/shard_map/ppermute | solution.py:22
  83.2 7.9 %collective-permute-start.11 = (f32[8,1,128]{2,0,1:T(8,128)S(1)}, f32[8,1,128]{2,0,1:T(8,128)S(1)}, u32[]{:S(2)}, u32[]{:S(2)}) collective-permute-start(f32[8,1,128]{2,0,1:T(8,128)S(1)} %get-tuple-element.23), channel_id=1, source_target_pairs={{1,0},{2,1},{3,2},{4,3},{5,4},{6,5},{7,6},{8,7},{9,8},{10,9},{11,1... | collective-permute-start | bytes 12296 | tf_op jit(solution)/shard_map/ppermute | solution.py:35
  84.5 6.6 %collective-permute-start.10 = (f32[8,1,128]{2,0,1:T(8,128)S(1)}, f32[8,1,128]{2,0,1:T(8,128)S(1)}, u32[]{:S(2)}, u32[]{:S(2)}) collective-permute-start(f32[8,1,128]{2,0,1:T(8,128)S(1)} %get-tuple-element.23), channel_id=1, source_target_pairs={{0,1},{1,2},{2,3},{3,4},{4,5},{5,6},{6,7},{7,8},{8,9},{9,10},{10,1... | collective-permute-start | bytes 12296 | tf_op jit(solution)/shard_map/ppermute | solution.py:33
  111.3 12.6 %all-to-all-start.3 = ((f32[8,16,100]{2,0,1:T(8,128)}), f32[8,16,100]{2,0,1:T(8,128)S(1)}, u32[]{:S(2)}, u32[]{:S(2)}) async-start(f32[8,16,100]{2,0,1:T(8,128)} %copy.42), calls=%async_computation.3 | async-start | bytes 131072 | tf_op jit(solution)/shard_map/all_to_all | solution.py:79
